TPU v7x, 32 devices: a whole 2x2x4 slice. The times are simulated.
32 devices in a mesh: groups: 2 (over x), face: 8 (over z, y), sub: 2 (over core).
Axes of the slice: x: 2, y: 2, z: 4, core: 2. Of those that a mesh axis runs over, the one named last changes fastest.
Arguments:
- features: bfloat16 [65536, 64], P(('groups', 'face', 'sub')), parts along dimension 0
- links_fine: int32 [9, 32768], P(None, ('face', 'sub')), may hold values from 0 to 2175, as said below
- sends_fine: int32 [16, 2, 64], P(('face', 'sub')), may hold values from 0 to 2047, as said below
- links_mid: int32 [9, 8192], P(None, ('face', 'sub')), may hold values from 0 to 575, as said below
- sends_mid: int32 [16, 2, 32], P(('face', 'sub')), may hold values from 0 to 511, as said below
- links_coarse: int32 [9, 2048], P(None, ('face', 'sub')), may hold values from 0 to 159, as said below
- sends_coarse: int32 [16, 2, 16], P(('face', 'sub')), may hold values from 0 to 127, as said below
- kernel_enter: bfloat16 [9, 64, 128], replicated, may hold values from -0.25 to 0.25
- gain_enter: float32 [128], replicated, may hold values from 0.5 to 1.5
- shift_enter: float32 [128], replicated, may hold values from -2.5 to 2.5
- kernel_fine: bfloat16 [9, 128, 128], replicated, may hold values from -0.1875 to 0.1875
- gain_fine: float32 [128], replicated, may hold values from 0.5 to 1.5
- shift_fine: float32 [128], replicated, may hold values from -2.5 to 2.5
- kernel_widen: bfloat16 [9, 128, 256], replicated, may hold values from -0.1875 to 0.1875
- gain_widen: float32 [256], replicated, may hold values from 0.5 to 1.5
- shift_widen: float32 [256], replicated, may hold values from -2.5 to 2.5
- kernel_mid: bfloat16 [9, 256, 256], replicated, may hold values from -0.125 to 0.125
- gain_mid: float32 [256], replicated, may hold values from 0.5 to 1.5
- shift_mid: float32 [256], replicated, may hold values from -2.5 to 2.5
- kernel_deep: bfloat16 [9, 256, 512], replicated, may hold values from -0.125 to 0.125
- gain_deep: float32 [512], replicated, may hold values from 0.5 to 1.5
- shift_deep: float32 [512], replicated, may hold values from -2.5 to 2.5
Outputs:
- skip_fine: bfloat16 [65536, 128], P(('groups', 'face', 'sub')), parts along dimension 0
- skip_mid: bfloat16 [16384, 256], P(('groups', 'face', 'sub')), parts along dimension 0
- bottleneck: bfloat16 [4096, 512], P(('groups', 'face', 'sub')), parts along dimension 0
There are 2 independent parts, one for each index of `groups`. A program takes and returns all parts, laid end to end along the dimension named above; an argument that names none is the same for every part. Nothing has to cross between parts.
Inputs may be any that keep to these rules, and one draw needn't show every extreme that they name: links_fine[0, p] is p's own row within its range; every entry below 2048 is a row of the own range, entries from 2048 on index the padded block's received rows. sends_fine[g, 0] lists range g's first 64 rows in some order, sends_fine[g, 1] its last 64 rows in some order. links_mid[0, p] is p's own row within its range; entries from 512 on index the padded block's received rows. sends_mid[g, 0] lists range g's first 32 rows in some order, sends_mid[g, 1] its last 32 rows in some order. links_coarse[0, p] is p's own row within its range; entries from 128 on index the padded block's received rows. sends_coarse[g, 0] lists range g's first 16 rows in some order, sends_coarse[g, 1] its last 16 rows in some order.
All inputs are finite; a program needn't handle non-finite values.
Results may differ from a plain program's by a relative error of at most 0.011.
Values may be sent and summed in bfloat16 or wider, within the bound.
No kernel may reach another device: no remote copies, remote signals or barrier semaphores. Data moves between devices by JAX's collectives and lax.ppermute only.
A program may use at most 64 MiB of HBM per device.

v0:
```python
import jax
import jax.numpy as jnp
from jax import lax
from jax.sharding import PartitionSpec as P


def shifted(value, axis, steps):
    count = lax.axis_size(axis)
    pairs = [(source, (source + steps) % count) for source in range(count)]
    return lax.ppermute(value, axis, pairs)


def unchanged(vector):
    return vector


def pad_block(feat, sends):
    to_left = feat[sends[0, 0]]
    to_right = feat[sends[0, 1]]
    from_left = shifted(to_right, ("face", "sub"), 1)
    from_right = shifted(to_left, ("face", "sub"), -1)
    return jnp.concatenate([feat, from_left, from_right], axis=0)


def convolve(feat, sends, links, kernel):
    padded = pad_block(feat, sends)
    total = jnp.zeros((feat.shape[0], kernel.shape[2]), jnp.float32)
    for tap in range(9):
        total = total + jnp.dot(padded[links[tap]], kernel[tap], preferred_element_type=jnp.float32)
    return total


def normalize(total, gain, shift, count, spread, pick):
    summed = lax.psum(spread(jnp.sum(total, axis=0)), ("face", "sub"))
    mean = pick(summed) / count
    centered = total - mean
    squared = lax.psum(spread(jnp.sum(centered * centered, axis=0)), ("face", "sub"))
    var = pick(squared) / count
    normed = centered * lax.rsqrt(var + 1e-05) * gain + shift
    return jax.nn.gelu(normed, approximate=False).astype(jnp.bfloat16)


def pooling(act):
    return jnp.mean(act.reshape(-1, 4, act.shape[1]).astype(jnp.float32), axis=1).astype(
        jnp.bfloat16
    )


def sharded_layer(feat, sends, links, kernel, gain, shift):
    total = convolve(feat, sends, links, kernel)
    count = float(total.shape[0] * lax.axis_size("face") * lax.axis_size("sub"))
    return normalize(total, gain, shift, count, unchanged, unchanged)


def per_device(
    features,
    links_fine,
    sends_fine,
    links_mid,
    sends_mid,
    links_coarse,
    sends_coarse,
    kernel_enter,
    gain_enter,
    shift_enter,
    kernel_fine,
    gain_fine,
    shift_fine,
    kernel_widen,
    gain_widen,
    shift_widen,
    kernel_mid,
    gain_mid,
    shift_mid,
    kernel_deep,
    gain_deep,
    shift_deep,
):
    first_fine = sharded_layer(
        features, sends_fine, links_fine, kernel_enter, gain_enter, shift_enter
    )
    skip_fine = sharded_layer(
        first_fine, sends_fine, links_fine, kernel_fine, gain_fine, shift_fine
    )
    pooled_mid = pooling(skip_fine)
    first_mid = sharded_layer(
        pooled_mid, sends_mid, links_mid, kernel_widen, gain_widen, shift_widen
    )
    skip_mid = sharded_layer(first_mid, sends_mid, links_mid, kernel_mid, gain_mid, shift_mid)
    pooled_coarse = pooling(skip_mid)
    bottleneck = sharded_layer(
        pooled_coarse, sends_coarse, links_coarse, kernel_deep, gain_deep, shift_deep
    )
    return (skip_fine, skip_mid, bottleneck)


def solution(mesh):
    return jax.shard_map(
        per_device,
        mesh=mesh,
        in_specs=(
            P(("groups", "face", "sub"), None),
            P(None, ("face", "sub")),
            P(("face", "sub"), None, None),
            P(None, ("face", "sub")),
            P(("face", "sub"), None, None),
            P(None, ("face", "sub")),
            P(("face", "sub"), None, None),
            P(),
            P(),
            P(),
            P(),
            P(),
            P(),
            P(),
            P(),
            P(),
            P(),
            P(),
            P(),
            P(),
            P(),
            P(),
        ),
        out_specs=(
            P(("groups", "face", "sub"), None),
            P(("groups", "face", "sub"), None),
            P(("groups", "face", "sub"), None),
        ),
        check_vma=False,
    )
```

profile of v0, /device:TPU:0, one launch (start us, length us, event | category | flops | bytes accessed | tf_op | source)
XLA Modules:
  0.0 590.2 jit_solution(10003050943090886935)
XLA Ops:
  4.5 5.0 collective-permute-start.1
  9.6 1.4 compare_select_fusion.8
  14.8 6.2 %gather_fusion.10 = bf16[2048,64]{1,0:T(8,128)(2,1)S(1)} fusion(bf16[2176,64]{1,0:T(8,128)(2,1)S(1)} %pad_maximum_fusion, s32[2048]{0:T(1024)S(1)} %broadcast_clamp_fusion), kind=kCustom, calls=%fused_computation.10 | custom fusion | bytes 532480 | tf_op jit(solution)/shard_map/gather | solution.py:29
  21.0 8.1 %gather_fusion.9 = bf16[2048,64]{1,0:T(8,128)(2,1)} fusion(bf16[2176,64]{1,0:T(8,128)(2,1)S(1)} %pad_maximum_fusion, s32[2048]{0:T(1024)S(1)} %broadcast_clamp_fusion.1), kind=kCustom, calls=%fused_computation.9 | custom fusion | bytes 532480 | tf_op jit(solution)/shard_map/gather | solution.py:29
  30.4 8.1 %gather_fusion.8 = bf16[2048,64]{1,0:T(8,128)(2,1)} fusion(bf16[2176,64]{1,0:T(8,128)(2,1)S(1)} %pad_maximum_fusion, s32[2048]{0:T(1024)S(1)} %broadcast_clamp_fusion.2), kind=kCustom, calls=%fused_computation.8 | custom fusion | bytes 532480 | tf_op jit(solution)/shard_map/gather | solution.py:29
  38.4 2.3 fusion.193
  40.7 8.0 %gather_fusion.7 = bf16[2048,64]{1,0:T(8,128)(2,1)} fusion(bf16[2176,64]{1,0:T(8,128)(2,1)S(1)} %pad_maximum_fusion, s32[2048]{0:T(1024)S(1)} %broadcast_clamp_fusion.3), kind=kCustom, calls=%fused_computation.7 | custom fusion | bytes 532480 | tf_op jit(solution)/shard_map/gather | solution.py:29
  48.8 2.3 fusion.195
  51.1 8.0 %gather_fusion.6 = bf16[2048,64]{1,0:T(8,128)(2,1)} fusion(bf16[2176,64]{1,0:T(8,128)(2,1)S(1)} %pad_maximum_fusion, s32[2048]{0:T(1024)S(1)} %broadcast_clamp_fusion.4), kind=kCustom, calls=%fused_computation.6 | custom fusion | bytes 532480 | tf_op jit(solution)/shard_map/gather | solution.py:29
  59.1 2.3 fusion.197
  61.4 8.0 %gather_fusion.5 = bf16[2048,64]{1,0:T(8,128)(2,1)} fusion(bf16[2176,64]{1,0:T(8,128)(2,1)S(1)} %pad_maximum_fusion, s32[2048]{0:T(1024)S(1)} %broadcast_clamp_fusion.5), kind=kCustom, calls=%fused_computation.5 | custom fusion | bytes 532480 | tf_op jit(solution)/shard_map/gather | solution.py:29
  69.5 2.3 fusion.199
  71.8 8.0 %gather_fusion.4 = bf16[2048,64]{1,0:T(8,128)(2,1)} fusion(bf16[2176,64]{1,0:T(8,128)(2,1)S(1)} %pad_maximum_fusion, s32[2048]{0:T(1024)S(1)} %broadcast_clamp_fusion.6), kind=kCustom, calls=%fused_computation.4 | custom fusion | bytes 532480 | tf_op jit(solution)/shard_map/gather | solution.py:29
  79.8 2.3 fusion.201
  82.1 8.0 %gather_fusion.3 = bf16[2048,64]{1,0:T(8,128)(2,1)} fusion(bf16[2176,64]{1,0:T(8,128)(2,1)S(1)} %pad_maximum_fusion, s32[2048]{0:T(1024)S(1)} %broadcast_clamp_fusion.7), kind=kCustom, calls=%fused_computation.3 | custom fusion | bytes 532480 | tf_op jit(solution)/shard_map/gather | solution.py:29
  90.1 2.3 fusion.203
  92.5 8.0 %gather_fusion.2 = bf16[2048,64]{1,0:T(8,128)(2,1)} fusion(bf16[2176,64]{1,0:T(8,128)(2,1)S(1)} %pad_maximum_fusion, s32[2048]{0:T(1024)S(1)} %broadcast_clamp_fusion.8), kind=kCustom, calls=%fused_computation.2 | custom fusion | bytes 532480 | tf_op jit(solution)/shard_map/gather | solution.py:29
  100.5 3.5 fusion.230
  104.0 30.2 %psum.70 = f32[128]{0:T(128)S(1)} all-reduce(f32[128]{0:T(128)S(1)} %get-tuple-element.36), channel_id=1, replica_groups=mesh['groups'=2,'face'=8,'sub'=2] {'face','sub'}, use_global_device_ids=true, to_apply=%region_1.0 | all-reduce | flops 128 | bytes 1024 | tf_op jit(solution)/shard_map/psum | solution.py:34
  134.5 29.5 %psum.71 = f32[128]{0:T(128)S(1)} all-reduce(f32[128]{0:T(128)S(1)} %multiply_reduce_fusion.1), channel_id=1, replica_groups=mesh['groups'=2,'face'=8,'sub'=2] {'face','sub'}, use_global_device_ids=true, to_apply=%region_3.0 | all-reduce | flops 128 | bytes 1024 | tf_op jit(solution)/shard_map/psum | solution.py:37
  164.0 2.4 fusion.37
  167.8 4.4 collective-permute-start.3
  172.2 1.4 collective-permute-done.2
  173.7 6.2 %gather_fusion.20 = bf16[2048,128]{1,0:T(8,128)(2,1)S(1)} fusion(bf16[2176,128]{1,0:T(8,128)(2,1)S(1)} %pad_maximum_fusion.1, s32[2048]{0:T(1024)S(1)} %broadcast_clamp_fusion.1), kind=kCustom, calls=%fused_computation.20 | custom fusion | bytes 1056768 | tf_op jit(solution)/shard_map/gather | solution.py:29
  179.9 6.2 %gather_fusion.19 = bf16[2048,128]{1,0:T(8,128)(2,1)S(1)} fusion(bf16[2176,128]{1,0:T(8,128)(2,1)S(1)} %pad_maximum_fusion.1, s32[2048]{0:T(1024)S(1)} %broadcast_clamp_fusion.2), kind=kCustom, calls=%fused_computation.19 | custom fusion | bytes 1056768 | tf_op jit(solution)/shard_map/gather | solution.py:29
  186.1 6.2 %gather_fusion.18 = bf16[2048,128]{1,0:T(8,128)(2,1)S(1)} fusion(bf16[2176,128]{1,0:T(8,128)(2,1)S(1)} %pad_maximum_fusion.1, s32[2048]{0:T(1024)S(1)} %broadcast_clamp_fusion.3), kind=kCustom, calls=%fused_computation.18 | custom fusion | bytes 1056768 | tf_op jit(solution)/shard_map/gather | solution.py:29
  192.3 8.0 %gather_fusion.17 = bf16[2048,128]{1,0:T(8,128)(2,1)} fusion(bf16[2176,128]{1,0:T(8,128)(2,1)S(1)} %pad_maximum_fusion.1, s32[2048]{0:T(1024)S(1)} %broadcast_clamp_fusion.4), kind=kCustom, calls=%fused_computation.17 | custom fusion | bytes 1056768 | tf_op jit(solution)/shard_map/gather | solution.py:29
  200.3 8.0 %gather_fusion.16 = bf16[2048,128]{1,0:T(8,128)(2,1)} fusion(bf16[2176,128]{1,0:T(8,128)(2,1)S(1)} %pad_maximum_fusion.1, s32[2048]{0:T(1024)S(1)} %broadcast_clamp_fusion.5), kind=kCustom, calls=%fused_computation.16 | custom fusion | bytes 1056768 | tf_op jit(solution)/shard_map/gather | solution.py:29
  208.2 8.0 %gather_fusion.15 = bf16[2048,128]{1,0:T(8,128)(2,1)} fusion(bf16[2176,128]{1,0:T(8,128)(2,1)S(1)} %pad_maximum_fusion.1, s32[2048]{0:T(1024)S(1)} %broadcast_clamp_fusion.6), kind=kCustom, calls=%fused_computation.15 | custom fusion | bytes 1056768 | tf_op jit(solution)/shard_map/gather | solution.py:29
  216.2 8.0 %gather_fusion.14 = bf16[2048,128]{1,0:T(8,128)(2,1)} fusion(bf16[2176,128]{1,0:T(8,128)(2,1)S(1)} %pad_maximum_fusion.1, s32[2048]{0:T(1024)S(1)} %broadcast_clamp_fusion.7), kind=kCustom, calls=%fused_computation.14 | custom fusion | bytes 1056768 | tf_op jit(solution)/shard_map/gather | solution.py:29
  224.2 8.0 %gather_fusion.21 = bf16[2048,128]{1,0:T(8,128)(2,1)} fusion(bf16[2176,128]{1,0:T(8,128)(2,1)S(1)} %pad_maximum_fusion.1, s32[2048]{0:T(1024)S(1)} %broadcast_clamp_fusion), kind=kCustom, calls=%fused_computation.21 | custom fusion | bytes 1056768 | tf_op jit(solution)/shard_map/gather | solution.py:29
  232.2 6.2 %gather_fusion.13 = bf16[2048,128]{1,0:T(8,128)(2,1)S(1)} fusion(bf16[2176,128]{1,0:T(8,128)(2,1)S(1)} %pad_maximum_fusion.1, s32[2048]{0:T(1024)S(1)} %broadcast_clamp_fusion.8), kind=kCustom, calls=%fused_computation.13 | custom fusion | bytes 1056768 | tf_op jit(solution)/shard_map/gather | solution.py:29
  245.0 33.9 %psum.72 = f32[128]{0:T(128)S(1)} all-reduce(f32[128]{0:T(128)S(1)} %get-tuple-element.38), channel_id=1, replica_groups=mesh['groups'=2,'face'=8,'sub'=2] {'face','sub'}, use_global_device_ids=true, to_apply=%region_5.0 | all-reduce | flops 128 | bytes 1024 | tf_op jit(solution)/shard_map/psum | solution.py:34
  279.2 29.7 %psum.73 = f32[128]{0:T(128)S(1)} all-reduce(f32[128]{0:T(128)S(1)} %multiply_reduce_fusion), channel_id=1, replica_groups=mesh['groups'=2,'face'=8,'sub'=2] {'face','sub'}, use_global_device_ids=true, to_apply=%region_7.0 | all-reduce | flops 128 | bytes 1024 | tf_op jit(solution)/shard_map/psum | solution.py:37
  308.9 2.4 fusion.40
  313.4 4.5 collective-permute-start.5
  319.2 1.3 gather_fusion.32
  320.6 1.3 gather_fusion.31
  324.1 1.3 gather_fusion.30
  326.5 1.3 gather_fusion.29
  328.9 1.3 gather_fusion.28
  331.3 1.3 gather_fusion.27
  332.6 1.8 fusion.147
  335.8 1.9 fusion.149
  339.0 1.9 fusion.151
  342.2 1.7 fusion.232
  344.0 33.9 %psum.74 = f32[256]{0:T(256)S(1)} all-reduce(f32[256]{0:T(256)S(1)} %get-tuple-element.40), channel_id=1, replica_groups=mesh['groups'=2,'face'=8,'sub'=2] {'face','sub'}, use_global_device_ids=true, to_apply=%region_10.0 | all-reduce | flops 256 | bytes 2048 | tf_op jit(solution)/shard_map/psum | solution.py:34
  378.0 29.5 %psum.75 = f32[256]{0:T(256)S(1)} all-reduce(f32[256]{0:T(256)S(1)} %multiply_reduce_fusion.3), channel_id=1, replica_groups=mesh['groups'=2,'face'=8,'sub'=2] {'face','sub'}, use_global_device_ids=true, to_apply=%region_12.0 | all-reduce | flops 256 | bytes 2048 | tf_op jit(solution)/shard_map/psum | solution.py:37
  410.0 4.4 collective-permute-start.7
  415.9 2.0 gather_fusion.42
  417.9 2.0 gather_fusion.41
  419.9 2.0 gather_fusion.40
  421.8 2.0 gather_fusion.39
  423.8 2.0 gather_fusion.38
  425.7 2.0 gather_fusion.37
  427.7 2.6 gather_fusion.36
  430.3 2.6 gather_fusion.43
  432.9 1.9 gather_fusion.35
  437.3 33.9 %psum.76 = f32[256]{0:T(256)S(1)} all-reduce(f32[256]{0:T(256)S(1)} %get-tuple-element.42), channel_id=1, replica_groups=mesh['groups'=2,'face'=8,'sub'=2] {'face','sub'}, use_global_device_ids=true, to_apply=%region_14.0 | all-reduce | flops 256 | bytes 2048 | tf_op jit(solution)/shard_map/psum | solution.py:34
  471.3 29.5 %psum.77 = f32[256]{0:T(256)S(1)} all-reduce(f32[256]{0:T(256)S(1)} %multiply_reduce_fusion.2), channel_id=1, replica_groups=mesh['groups'=2,'face'=8,'sub'=2] {'face','sub'}, use_global_device_ids=true, to_apply=%region_16.0 | all-reduce | flops 256 | bytes 2048 | tf_op jit(solution)/shard_map/psum | solution.py:37
  504.2 4.7 collective-permute-start.9
  524.0 1.5 fusion.234
  525.5 33.9 %psum.78 = f32[512]{0:T(512)S(1)} all-reduce(f32[512]{0:T(512)S(1)} %get-tuple-element.44), channel_id=1, replica_groups=mesh['groups'=2,'face'=8,'sub'=2] {'face','sub'}, use_global_device_ids=true, to_apply=%region_19.0 | all-reduce | flops 512 | bytes 4096 | tf_op jit(solution)/shard_map/psum | solution.py:34
  559.5 29.5 %psum.79 = f32[512]{0:T(512)S(1)} all-reduce(f32[512]{0:T(512)S(1)} %multiply_reduce_fusion.4), channel_id=1, replica_groups=mesh['groups'=2,'face'=8,'sub'=2] {'face','sub'}, use_global_device_ids=true, to_apply=%region_21.0 | all-reduce | flops 512 | bytes 4096 | tf_op jit(solution)/shard_map/psum | solution.py:37
  (194 shorter events, 56.3 us)
Async XLA Ops:
  0.6 10.4 %copy-start.25 = (s32[1,2,32]{2,1,0:T(2,128)S(1)}, s32[1,2,32]{2,1,0:T(2,128)}, u32[]{:S(2)}) copy-start(s32[1,2,32]{2,1,0:T(2,128)} %param.26) | copy-start | bytes 772
  0.6 10.4 %copy-start.14 = (s32[9,512]{1,0:T(8,128)S(1)}, s32[9,512]{1,0:T(8,128)}, u32[]{:S(2)}) copy-start(s32[9,512]{1,0:T(8,128)} %param.25) | copy-start | bytes 55300
  0.7 10.6 %copy-start.26 = (s32[1,2,16]{2,1,0:T(2,128)S(1)}, s32[1,2,16]{2,1,0:T(2,128)}, u32[]{:S(2)}) copy-start(s32[1,2,16]{2,1,0:T(2,128)} %param.28) | copy-start | bytes 388
  0.7 11.1 %copy-start.15 = (s32[9,128]{1,0:T(8,128)S(1)}, s32[9,128]{1,0:T(8,128)}, u32[]{:S(2)}) copy-start(s32[9,128]{1,0:T(8,128)} %param.27) | copy-start | bytes 13828
  3.3 11.3 %collective-permute-start = (bf16[64,64]{1,0:T(8,128)(2,1)S(1)}, bf16[64,64]{1,0:T(8,128)(2,1)S(1)}, u32[]{:S(2)}, u32[]{:S(2)}) collective-permute-start(bf16[64,64]{1,0:T(8,128)(2,1)S(1)} %gather_fusion), channel_id=1, source_target_pairs={{0,1},{1,2},{2,3},{3,4},{4,5},{5,6},{6,7},{7,8},{8,9},{9,10},{10,1... | collective-permute-start | bytes 24584 | tf_op jit(solution)/shard_map/ppermute | solution.py:10
  4.5 10.2 %collective-permute-start.1 = (bf16[64,64]{1,0:T(8,128)(2,1)S(1)}, bf16[64,64]{1,0:T(8,128)(2,1)S(1)}, u32[]{:S(2)}, u32[]{:S(2)}) collective-permute-start(bf16[64,64]{1,0:T(8,128)(2,1)S(1)} %gather_fusion.1), channel_id=1, source_target_pairs={{0,15},{1,0},{2,1},{3,2},{4,3},{5,4},{6,5},{7,6},{8,7},{9,8},{10,9... | collective-permute-start | bytes 24584 | tf_op jit(solution)/shard_map/ppermute | solution.py:10
  21.0 8.1 %copy-start.13 = (bf16[9,64,128]{2,1,0:T(8,128)(2,1)S(1)}, bf16[9,64,128]{2,1,0:T(8,128)(2,1)}, u32[]{:S(2)}) copy-start(bf16[9,64,128]{2,1,0:T(8,128)(2,1)} %param.29) | copy-start | bytes 442372
  29.1 1.0 copy-start.6
  100.5 63.5 %copy-start.27 = (f32[128]{0:T(128)S(1)}, f32[128]{0:T(128)}, u32[]{:S(2)}) copy-start(f32[128]{0:T(128)} %param.31) | copy-start | bytes 1540
  100.5 63.5 %copy-start.28 = (f32[128]{0:T(128)S(1)}, f32[128]{0:T(128)}, u32[]{:S(2)}) copy-start(f32[128]{0:T(128)} %param.30) | copy-start | bytes 1540
  167.7 5.9 %collective-permute-start.2 = (bf16[64,128]{1,0:T(8,128)(2,1)S(1)}, bf16[64,128]{1,0:T(8,128)(2,1)S(1)}, u32[]{:S(2)}, u32[]{:S(2)}) collective-permute-start(bf16[64,128]{1,0:T(8,128)(2,1)S(1)} %gather_fusion.11), channel_id=1, source_target_pairs={{0,1},{1,2},{2,3},{3,4},{4,5},{5,6},{6,7},{7,8},{8,9},{9,10},{10,1... | collective-permute-start | bytes 49160 | tf_op jit(solution)/shard_map/ppermute | solution.py:10
  167.8 5.9 collective-permute-start.3
  232.2 6.2 %copy-start.12 = (bf16[9,128,128]{2,1,0:T(8,128)(2,1)S(1)}, bf16[9,128,128]{2,1,0:T(8,128)(2,1)}, u32[]{:S(2)}) copy-start(bf16[9,128,128]{2,1,0:T(8,128)(2,1)} %param.32) | copy-start | bytes 884740
  239.0 1.0 copy-start.1
  240.0 1.0 copy-start.2
  241.0 1.0 copy-start.3
  242.1 1.0 copy-start.4
  243.1 1.0 copy-start.5
  244.4 64.5 %copy-start.29 = (f32[128]{0:T(128)S(1)}, f32[128]{0:T(128)}, u32[]{:S(2)}) copy-start(f32[128]{0:T(128)} %param.34) | copy-start | bytes 1540
  244.5 64.4 %copy-start.30 = (f32[128]{0:T(128)S(1)}, f32[128]{0:T(128)}, u32[]{:S(2)}) copy-start(f32[128]{0:T(128)} %param.33) | copy-start | bytes 1540
  308.9 9.0 %copy-start.20 = (s32[16]{0:T(128)S(1)}, s32[16]{0:T(128)}, u32[]{:S(2)}) copy-start(s32[16]{0:T(128)} %get-tuple-element.30) | copy-start | bytes 196
  311.4 9.2 %copy-start.7 = (bf16[2048,128]{1,0:T(8,128)(2,1)}, bf16[2048,128]{1,0:T(8,128)(2,1)S(1)}, u32[]{:S(2)}) copy-start(bf16[2048,128]{1,0:T(8,128)(2,1)S(1)} %fusion.40) | copy-start | bytes 1572868
  312.7 5.8 collective-permute-start.4
  313.4 5.8 collective-permute-start.5
  342.2 65.3 %copy-start.21 = (f32[256]{0:T(256)S(1)}, f32[256]{0:T(256)}, u32[]{:S(2)}) copy-start(f32[256]{0:T(256)} %param.37) | copy-start | bytes 3076
  342.2 65.3 %copy-start.22 = (f32[256]{0:T(256)S(1)}, f32[256]{0:T(256)}, u32[]{:S(2)}) copy-start(f32[256]{0:T(256)} %param.36) | copy-start | bytes 3076
  344.0 70.5 %copy-start.19 = (s32[16]{0:T(128)S(1)}, s32[16]{0:T(128)}, u32[]{:S(2)}) copy-start(s32[16]{0:T(128)} %get-tuple-element.31) | copy-start | bytes 196
  410.0 5.9 %collective-permute-start.6 = (bf16[32,256]{1,0:T(8,128)(2,1)S(1)}, bf16[32,256]{1,0:T(8,128)(2,1)S(1)}, u32[]{:S(2)}, u32[]{:S(2)}) collective-permute-start(bf16[32,256]{1,0:T(8,128)(2,1)S(1)} %gather_fusion.33), channel_id=1, source_target_pairs={{0,1},{1,2},{2,3},{3,4},{4,5},{5,6},{6,7},{7,8},{8,9},{9,10},{10,1... | collective-permute-start | bytes 49160 | tf_op jit(solution)/shard_map/ppermute | solution.py:10
  410.0 5.9 collective-permute-start.7
  432.8 2.0 copy-start.8
  435.5 1.0 copy-start.10
  435.7 1.0 copy-start.11
  436.9 63.9 %copy-start.23 = (f32[256]{0:T(256)S(1)}, f32[256]{0:T(256)}, u32[]{:S(2)}) copy-start(f32[256]{0:T(256)} %param.40) | copy-start | bytes 3076
  436.9 63.9 %copy-start.24 = (f32[256]{0:T(256)S(1)}, f32[256]{0:T(256)}, u32[]{:S(2)}) copy-start(f32[256]{0:T(256)} %param.39) | copy-start | bytes 3076
  500.8 8.1 %copy-start.18 = (s32[128]{0:T(128)S(1)}, s32[128]{0:T(128)}, u32[]{:S(2)}) copy-start(s32[128]{0:T(128)} %get-tuple-element.21) | copy-start | bytes 1540
  502.1 9.2 %copy-start.9 = (bf16[512,256]{1,0:T(8,128)(2,1)}, bf16[512,256]{1,0:T(8,128)(2,1)S(1)}, u32[]{:S(2)}) copy-start(bf16[512,256]{1,0:T(8,128)(2,1)S(1)} %fusion.60) | copy-start | bytes 786436
  502.1 10.2 %copy-start = (bf16[9,256,512]{2,1,0:T(8,128)(2,1)S(1)}, bf16[9,256,512]{2,1,0:T(8,128)(2,1)}, u32[]{:S(2)}) copy-start(bf16[9,256,512]{2,1,0:T(8,128)(2,1)} %param.41) | copy-start | bytes 7077892
  503.4 5.8 collective-permute-start.8
  504.2 6.1 %collective-permute-start.9 = (bf16[16,256]{1,0:T(8,128)(2,1)S(1)}, bf16[16,256]{1,0:T(8,128)(2,1)S(1)}, u32[]{:S(2)}, u32[]{:S(2)}) collective-permute-start(bf16[16,256]{1,0:T(8,128)(2,1)S(1)} %gather_fusion.45), channel_id=1, source_target_pairs={{0,15},{1,0},{2,1},{3,2},{4,3},{5,4},{6,5},{7,6},{8,7},{9,8},{10,9... | collective-permute-start | bytes 24584 | tf_op jit(solution)/shard_map/ppermute | solution.py:10
  524.0 65.0 %copy-start.16 = (f32[512]{0:T(512)S(1)}, f32[512]{0:T(512)}, u32[]{:S(2)}) copy-start(f32[512]{0:T(512)} %param.43) | copy-start | bytes 6148
  524.0 65.0 %copy-start.17 = (f32[512]{0:T(512)S(1)}, f32[512]{0:T(512)}, u32[]{:S(2)}) copy-start(f32[512]{0:T(512)} %param.42) | copy-start | bytes 6148
where the time goes:
time: 592 us; the launch traced here: 590 us
  blocking collectives  313 us (53%)
  local copies, waits for them, and re-layouts  188 us (32%)
  matrix products  41.8 us (7%)
  starting transfers between devices  23.9 us (4%)
  other arithmetic  17.6 us (3%)
    gather x45, local copies, waits for them, and re-layouts, convolve(): padded[links[tap]]  175 us
    psum x5, blocking collectives, normalize(): summed = lax.psum(spread(jnp.sum(total, axis=0)), ('face', 'sub'))  166 us
    psum x5, blocking collectives, normalize(): lax.psum(spread(jnp.sum(centered * centered, axis=0)), ('face', 'sub'))  148 us
    dot_general x45, matrix products, convolve(): jnp.dot(padded[links[tap]], kernel[tap], preferred_element_type=jnp.float32)  41.8 us
    ppermute x10, starting transfers between devices, shifted(): return lax.ppermute(value, axis, pairs)  23.9 us
  transfers between devices with their start and end apart: 10, of which 6 were waited for; matrix products, arithmetic and copies ran while one was open for 1% of the time, Pallas kernels for 0%

commit v1 on v0

--- a/solution.py
+++ b/solution.py
@@ -31,7 +31,7 @@
 
 
 def normalize(total, gain, shift, count, spread, pick):
-    summed = lax.psum(spread(jnp.sum(total, axis=0)), ("face", "sub"))
+    summed = jnp.sum(lax.all_gather(spread(jnp.sum(total, axis=0)), ("face", "sub")), axis=0)
     mean = pick(summed) / count
     centered = total - mean
     squared = lax.psum(spread(jnp.sum(centered * centered, axis=0)), ("face", "sub"))

time: 592 us -> 523 us (0.88)
  blocking collectives: 313 us -> 244 us
    psum x5 -> x0, blocking collectives: 166 us -> none  [normalize(): summed = lax.psum(spread(jnp.sum(total, axis=0)), ('face', 'sub'))]
    all_gather x0 -> x5, blocking collectives: none -> 91.5 us  [normalize(): lax.all_gather(spread(jnp.sum(total, axis=0)), ('face', 'sub'))]
  transfers between devices with their start and end apart: 10 -> 10, of which waited for: 6 -> 6; matrix products, arithmetic and copies ran while one was open for 1% -> 2% of each run, Pallas kernels for 0% -> 0%
where the time goes in v1:
time: 523 us; the launch traced here: 521 us
  blocking collectives  244 us (47%)
  local copies, waits for them, and re-layouts  188 us (36%)
  matrix products  41.8 us (8%)
  starting transfers between devices  23.9 us (5%)
  other arithmetic  17.8 us (3%)
    gather x45, local copies, waits for them, and re-layouts, convolve(): padded[links[tap]]  175 us
    psum x5, blocking collectives, normalize(): lax.psum(spread(jnp.sum(centered * centered, axis=0)), ('face', 'sub'))  153 us
    all_gather x5, blocking collectives, normalize(): lax.all_gather(spread(jnp.sum(total, axis=0)), ('face', 'sub'))  91.5 us
    dot_general x45, matrix products, convolve(): jnp.dot(padded[links[tap]], kernel[tap], preferred_element_type=jnp.float32)  41.8 us
    ppermute x10, starting transfers between devices, shifted(): return lax.ppermute(value, axis, pairs)  23.9 us
  transfers between devices with their start and end apart: 10, of which 6 were waited for; matrix products, arithmetic and copies ran while one was open for 2% of the time, Pallas kernels for 0%

profile of v1, /device:TPU:0, one launch (start us, length us, event | category | flops | bytes accessed | tf_op | source)
XLA Modules:
  0.0 521.1 jit_solution(2677408576819039451)
XLA Ops:
  4.5 5.0 collective-permute-start.1
  9.6 1.4 compare_select_fusion.8
  14.8 6.2 %gather_fusion.10 = bf16[2048,64]{1,0:T(8,128)(2,1)S(1)} fusion(bf16[2176,64]{1,0:T(8,128)(2,1)S(1)} %pad_maximum_fusion, s32[2048]{0:T(1024)S(1)} %broadcast_clamp_fusion), kind=kCustom, calls=%fused_computation.10 | custom fusion | bytes 532480 | tf_op jit(solution)/shard_map/gather | solution.py:29
  21.0 8.1 %gather_fusion.9 = bf16[2048,64]{1,0:T(8,128)(2,1)} fusion(bf16[2176,64]{1,0:T(8,128)(2,1)S(1)} %pad_maximum_fusion, s32[2048]{0:T(1024)S(1)} %broadcast_clamp_fusion.1), kind=kCustom, calls=%fused_computation.9 | custom fusion | bytes 532480 | tf_op jit(solution)/shard_map/gather | solution.py:29
  30.4 8.1 %gather_fusion.8 = bf16[2048,64]{1,0:T(8,128)(2,1)} fusion(bf16[2176,64]{1,0:T(8,128)(2,1)S(1)} %pad_maximum_fusion, s32[2048]{0:T(1024)S(1)} %broadcast_clamp_fusion.2), kind=kCustom, calls=%fused_computation.8 | custom fusion | bytes 532480 | tf_op jit(solution)/shard_map/gather | solution.py:29
  38.4 2.3 fusion.193
  40.7 8.0 %gather_fusion.7 = bf16[2048,64]{1,0:T(8,128)(2,1)} fusion(bf16[2176,64]{1,0:T(8,128)(2,1)S(1)} %pad_maximum_fusion, s32[2048]{0:T(1024)S(1)} %broadcast_clamp_fusion.3), kind=kCustom, calls=%fused_computation.7 | custom fusion | bytes 532480 | tf_op jit(solution)/shard_map/gather | solution.py:29
  48.8 2.3 fusion.195
  51.1 8.0 %gather_fusion.6 = bf16[2048,64]{1,0:T(8,128)(2,1)} fusion(bf16[2176,64]{1,0:T(8,128)(2,1)S(1)} %pad_maximum_fusion, s32[2048]{0:T(1024)S(1)} %broadcast_clamp_fusion.4), kind=kCustom, calls=%fused_computation.6 | custom fusion | bytes 532480 | tf_op jit(solution)/shard_map/gather | solution.py:29
  59.1 2.3 fusion.197
  61.4 8.0 %gather_fusion.5 = bf16[2048,64]{1,0:T(8,128)(2,1)} fusion(bf16[2176,64]{1,0:T(8,128)(2,1)S(1)} %pad_maximum_fusion, s32[2048]{0:T(1024)S(1)} %broadcast_clamp_fusion.5), kind=kCustom, calls=%fused_computation.5 | custom fusion | bytes 532480 | tf_op jit(solution)/shard_map/gather | solution.py:29
  69.5 2.3 fusion.199
  71.8 8.0 %gather_fusion.4 = bf16[2048,64]{1,0:T(8,128)(2,1)} fusion(bf16[2176,64]{1,0:T(8,128)(2,1)S(1)} %pad_maximum_fusion, s32[2048]{0:T(1024)S(1)} %broadcast_clamp_fusion.6), kind=kCustom, calls=%fused_computation.4 | custom fusion | bytes 532480 | tf_op jit(solution)/shard_map/gather | solution.py:29
  79.8 2.3 fusion.201
  82.1 8.0 %gather_fusion.3 = bf16[2048,64]{1,0:T(8,128)(2,1)} fusion(bf16[2176,64]{1,0:T(8,128)(2,1)S(1)} %pad_maximum_fusion, s32[2048]{0:T(1024)S(1)} %broadcast_clamp_fusion.7), kind=kCustom, calls=%fused_computation.3 | custom fusion | bytes 532480 | tf_op jit(solution)/shard_map/gather | solution.py:29
  90.1 2.3 fusion.203
  92.5 8.0 %gather_fusion.2 = bf16[2048,64]{1,0:T(8,128)(2,1)} fusion(bf16[2176,64]{1,0:T(8,128)(2,1)S(1)} %pad_maximum_fusion, s32[2048]{0:T(1024)S(1)} %broadcast_clamp_fusion.8), kind=kCustom, calls=%fused_computation.2 | custom fusion | bytes 532480 | tf_op jit(solution)/shard_map/gather | solution.py:29
  100.5 3.5 fusion.230
  104.0 19.4 %all-gather.5 = f32[16,1,128]{2,1,0:T(1,128)S(1)} all-gather(f32[1,1,128]{2,1,0:T(1,128)S(1)} %bitcast.333), channel_id=2, replica_groups=mesh['groups'=2,'face'=8,'sub'=2] {'face','sub'}, dimensions={0}, use_global_device_ids=true | all-gather | bytes 8704 | tf_op jit(solution)/shard_map/all_gather | solution.py:34
  123.8 29.8 %psum.35 = f32[128]{0:T(128)S(1)} all-reduce(f32[128]{0:T(128)S(1)} %multiply_reduce_fusion.1), channel_id=1, replica_groups=mesh['groups'=2,'face'=8,'sub'=2] {'face','sub'}, use_global_device_ids=true, to_apply=%region_3.0 | all-reduce | flops 128 | bytes 1024 | tf_op jit(solution)/shard_map/psum | solution.py:37
  153.6 2.4 fusion.37
  157.4 4.4 collective-permute-start.3
  161.8 1.4 collective-permute-done.2
  163.3 6.2 %gather_fusion.20 = bf16[2048,128]{1,0:T(8,128)(2,1)S(1)} fusion(bf16[2176,128]{1,0:T(8,128)(2,1)S(1)} %pad_maximum_fusion.1, s32[2048]{0:T(1024)S(1)} %broadcast_clamp_fusion.1), kind=kCustom, calls=%fused_computation.20 | custom fusion | bytes 1056768 | tf_op jit(solution)/shard_map/gather | solution.py:29
  169.5 6.2 %gather_fusion.19 = bf16[2048,128]{1,0:T(8,128)(2,1)S(1)} fusion(bf16[2176,128]{1,0:T(8,128)(2,1)S(1)} %pad_maximum_fusion.1, s32[2048]{0:T(1024)S(1)} %broadcast_clamp_fusion.2), kind=kCustom, calls=%fused_computation.19 | custom fusion | bytes 1056768 | tf_op jit(solution)/shard_map/gather | solution.py:29
  175.7 6.2 %gather_fusion.18 = bf16[2048,128]{1,0:T(8,128)(2,1)S(1)} fusion(bf16[2176,128]{1,0:T(8,128)(2,1)S(1)} %pad_maximum_fusion.1, s32[2048]{0:T(1024)S(1)} %broadcast_clamp_fusion.3), kind=kCustom, calls=%fused_computation.18 | custom fusion | bytes 1056768 | tf_op jit(solution)/shard_map/gather | solution.py:29
  181.9 8.0 %gather_fusion.17 = bf16[2048,128]{1,0:T(8,128)(2,1)} fusion(bf16[2176,128]{1,0:T(8,128)(2,1)S(1)} %pad_maximum_fusion.1, s32[2048]{0:T(1024)S(1)} %broadcast_clamp_fusion.4), kind=kCustom, calls=%fused_computation.17 | custom fusion | bytes 1056768 | tf_op jit(solution)/shard_map/gather | solution.py:29
  189.8 8.0 %gather_fusion.16 = bf16[2048,128]{1,0:T(8,128)(2,1)} fusion(bf16[2176,128]{1,0:T(8,128)(2,1)S(1)} %pad_maximum_fusion.1, s32[2048]{0:T(1024)S(1)} %broadcast_clamp_fusion.5), kind=kCustom, calls=%fused_computation.16 | custom fusion | bytes 1056768 | tf_op jit(solution)/shard_map/gather | solution.py:29
  197.8 8.0 %gather_fusion.15 = bf16[2048,128]{1,0:T(8,128)(2,1)} fusion(bf16[2176,128]{1,0:T(8,128)(2,1)S(1)} %pad_maximum_fusion.1, s32[2048]{0:T(1024)S(1)} %broadcast_clamp_fusion.6), kind=kCustom, calls=%fused_computation.15 | custom fusion | bytes 1056768 | tf_op jit(solution)/shard_map/gather | solution.py:29
  205.8 8.0 %gather_fusion.14 = bf16[2048,128]{1,0:T(8,128)(2,1)} fusion(bf16[2176,128]{1,0:T(8,128)(2,1)S(1)} %pad_maximum_fusion.1, s32[2048]{0:T(1024)S(1)} %broadcast_clamp_fusion.7), kind=kCustom, calls=%fused_computation.14 | custom fusion | bytes 1056768 | tf_op jit(solution)/shard_map/gather | solution.py:29
  213.7 8.0 %gather_fusion.21 = bf16[2048,128]{1,0:T(8,128)(2,1)} fusion(bf16[2176,128]{1,0:T(8,128)(2,1)S(1)} %pad_maximum_fusion.1, s32[2048]{0:T(1024)S(1)} %broadcast_clamp_fusion), kind=kCustom, calls=%fused_computation.21 | custom fusion | bytes 1056768 | tf_op jit(solution)/shard_map/gather | solution.py:29
  221.8 6.2 %gather_fusion.13 = bf16[2048,128]{1,0:T(8,128)(2,1)S(1)} fusion(bf16[2176,128]{1,0:T(8,128)(2,1)S(1)} %pad_maximum_fusion.1, s32[2048]{0:T(1024)S(1)} %broadcast_clamp_fusion.8), kind=kCustom, calls=%fused_computation.13 | custom fusion | bytes 1056768 | tf_op jit(solution)/shard_map/gather | solution.py:29
  234.6 18.0 %all-gather.6 = f32[16,1,128]{2,1,0:T(1,128)S(1)} all-gather(f32[1,1,128]{2,1,0:T(1,128)S(1)} %bitcast.334), channel_id=3, replica_groups=mesh['groups'=2,'face'=8,'sub'=2] {'face','sub'}, dimensions={0}, use_global_device_ids=true | all-gather | bytes 8704 | tf_op jit(solution)/shard_map/all_gather | solution.py:34
  252.9 30.8 %psum.36 = f32[128]{0:T(128)S(1)} all-reduce(f32[128]{0:T(128)S(1)} %multiply_reduce_fusion), channel_id=1, replica_groups=mesh['groups'=2,'face'=8,'sub'=2] {'face','sub'}, use_global_device_ids=true, to_apply=%region_7.0 | all-reduce | flops 128 | bytes 1024 | tf_op jit(solution)/shard_map/psum | solution.py:37
  283.8 2.4 fusion.40
  288.2 4.5 collective-permute-start.5
  294.1 1.3 gather_fusion.32
  295.5 1.3 gather_fusion.31
  298.9 1.3 gather_fusion.30
  301.3 1.3 gather_fusion.29
  303.7 1.3 gather_fusion.28
  306.1 1.3 gather_fusion.27
  307.5 1.8 fusion.147
  310.6 1.9 fusion.149
  313.8 1.9 fusion.151
  317.1 1.7 fusion.232
  318.8 18.0 %all-gather.7 = f32[16,1,256]{2,1,0:T(1,128)S(1)} all-gather(f32[1,1,256]{2,1,0:T(1,128)S(1)} %bitcast.331), channel_id=4, replica_groups=mesh['groups'=2,'face'=8,'sub'=2] {'face','sub'}, dimensions={0}, use_global_device_ids=true | all-gather | bytes 17408 | tf_op jit(solution)/shard_map/all_gather | solution.py:34
  337.0 30.7 %psum.37 = f32[256]{0:T(256)S(1)} all-reduce(f32[256]{0:T(256)S(1)} %multiply_reduce_fusion.3), channel_id=1, replica_groups=mesh['groups'=2,'face'=8,'sub'=2] {'face','sub'}, use_global_device_ids=true, to_apply=%region_12.0 | all-reduce | flops 256 | bytes 2048 | tf_op jit(solution)/shard_map/psum | solution.py:37
  370.2 4.4 collective-permute-start.7
  376.1 2.0 gather_fusion.42
  378.0 2.0 gather_fusion.41
  380.0 2.0 gather_fusion.40
  382.0 2.0 gather_fusion.39
  383.9 2.0 gather_fusion.38
  385.9 2.0 gather_fusion.37
  387.8 2.6 gather_fusion.36
  390.4 2.6 gather_fusion.43
  393.0 1.9 gather_fusion.35
  397.5 18.0 %all-gather.8 = f32[16,1,256]{2,1,0:T(1,128)S(1)} all-gather(f32[1,1,256]{2,1,0:T(1,128)S(1)} %bitcast.332), channel_id=5, replica_groups=mesh['groups'=2,'face'=8,'sub'=2] {'face','sub'}, dimensions={0}, use_global_device_ids=true | all-gather | bytes 17408 | tf_op jit(solution)/shard_map/all_gather | solution.py:34
  415.6 30.7 %psum.38 = f32[256]{0:T(256)S(1)} all-reduce(f32[256]{0:T(256)S(1)} %multiply_reduce_fusion.2), channel_id=1, replica_groups=mesh['groups'=2,'face'=8,'sub'=2] {'face','sub'}, use_global_device_ids=true, to_apply=%region_16.0 | all-reduce | flops 256 | bytes 2048 | tf_op jit(solution)/shard_map/psum | solution.py:37
  449.6 4.7 collective-permute-start.9
  469.5 1.5 fusion.234
  471.0 18.0 %all-gather.9 = f32[16,1,512]{2,1,0:T(1,128)S(1)} all-gather(f32[1,1,512]{2,1,0:T(1,128)S(1)} %bitcast.321), channel_id=6, replica_groups=mesh['groups'=2,'face'=8,'sub'=2] {'face','sub'}, dimensions={0}, use_global_device_ids=true | all-gather | bytes 34816 | tf_op jit(solution)/shard_map/all_gather | solution.py:34
  489.1 30.7 %psum.39 = f32[512]{0:T(512)S(1)} all-reduce(f32[512]{0:T(512)S(1)} %multiply_reduce_fusion.4), channel_id=1, replica_groups=mesh['groups'=2,'face'=8,'sub'=2] {'face','sub'}, use_global_device_ids=true, to_apply=%region_21.0 | all-reduce | flops 512 | bytes 4096 | tf_op jit(solution)/shard_map/psum | solution.py:37
  (199 shorter events, 56.5 us)
Async XLA Ops:
  0.6 10.4 %copy-start.25 = (s32[1,2,32]{2,1,0:T(2,128)S(1)}, s32[1,2,32]{2,1,0:T(2,128)}, u32[]{:S(2)}) copy-start(s32[1,2,32]{2,1,0:T(2,128)} %param.26) | copy-start | bytes 772
  0.6 10.4 %copy-start.14 = (s32[9,512]{1,0:T(8,128)S(1)}, s32[9,512]{1,0:T(8,128)}, u32[]{:S(2)}) copy-start(s32[9,512]{1,0:T(8,128)} %param.25) | copy-start | bytes 55300
  0.7 10.6 %copy-start.26 = (s32[1,2,16]{2,1,0:T(2,128)S(1)}, s32[1,2,16]{2,1,0:T(2,128)}, u32[]{:S(2)}) copy-start(s32[1,2,16]{2,1,0:T(2,128)} %param.28) | copy-start | bytes 388
  0.7 11.1 %copy-start.15 = (s32[9,128]{1,0:T(8,128)S(1)}, s32[9,128]{1,0:T(8,128)}, u32[]{:S(2)}) copy-start(s32[9,128]{1,0:T(8,128)} %param.27) | copy-start | bytes 13828
  3.3 11.3 %collective-permute-start = (bf16[64,64]{1,0:T(8,128)(2,1)S(1)}, bf16[64,64]{1,0:T(8,128)(2,1)S(1)}, u32[]{:S(2)}, u32[]{:S(2)}) collective-permute-start(bf16[64,64]{1,0:T(8,128)(2,1)S(1)} %gather_fusion), channel_id=1, source_target_pairs={{0,1},{1,2},{2,3},{3,4},{4,5},{5,6},{6,7},{7,8},{8,9},{9,10},{10,1... | collective-permute-start | bytes 24584 | tf_op jit(solution)/shard_map/ppermute | solution.py:10
  4.5 10.2 %collective-permute-start.1 = (bf16[64,64]{1,0:T(8,128)(2,1)S(1)}, bf16[64,64]{1,0:T(8,128)(2,1)S(1)}, u32[]{:S(2)}, u32[]{:S(2)}) collective-permute-start(bf16[64,64]{1,0:T(8,128)(2,1)S(1)} %gather_fusion.1), channel_id=1, source_target_pairs={{0,15},{1,0},{2,1},{3,2},{4,3},{5,4},{6,5},{7,6},{8,7},{9,8},{10,9... | collective-permute-start | bytes 24584 | tf_op jit(solution)/shard_map/ppermute | solution.py:10
  21.0 8.1 %copy-start.13 = (bf16[9,64,128]{2,1,0:T(8,128)(2,1)S(1)}, bf16[9,64,128]{2,1,0:T(8,128)(2,1)}, u32[]{:S(2)}) copy-start(bf16[9,64,128]{2,1,0:T(8,128)(2,1)} %param.29) | copy-start | bytes 442372
  29.1 1.0 copy-start.6
  100.5 53.1 %copy-start.27 = (f32[128]{0:T(128)S(1)}, f32[128]{0:T(128)}, u32[]{:S(2)}) copy-start(f32[128]{0:T(128)} %param.31) | copy-start | bytes 1540
  100.5 53.1 %copy-start.28 = (f32[128]{0:T(128)S(1)}, f32[128]{0:T(128)}, u32[]{:S(2)}) copy-start(f32[128]{0:T(128)} %param.30) | copy-start | bytes 1540
  157.3 5.9 %collective-permute-start.2 = (bf16[64,128]{1,0:T(8,128)(2,1)S(1)}, bf16[64,128]{1,0:T(8,128)(2,1)S(1)}, u32[]{:S(2)}, u32[]{:S(2)}) collective-permute-start(bf16[64,128]{1,0:T(8,128)(2,1)S(1)} %gather_fusion.11), channel_id=1, source_target_pairs={{0,1},{1,2},{2,3},{3,4},{4,5},{5,6},{6,7},{7,8},{8,9},{9,10},{10,1... | collective-permute-start | bytes 49160 | tf_op jit(solution)/shard_map/ppermute | solution.py:10
  157.4 5.9 %collective-permute-start.3 = (bf16[64,128]{1,0:T(8,128)(2,1)S(1)}, bf16[64,128]{1,0:T(8,128)(2,1)S(1)}, u32[]{:S(2)}, u32[]{:S(2)}) collective-permute-start(bf16[64,128]{1,0:T(8,128)(2,1)S(1)} %gather_fusion.12), channel_id=1, source_target_pairs={{0,15},{1,0},{2,1},{3,2},{4,3},{5,4},{6,5},{7,6},{8,7},{9,8},{10,9... | collective-permute-start | bytes 49160 | tf_op jit(solution)/shard_map/ppermute | solution.py:10
  221.8 6.2 %copy-start.12 = (bf16[9,128,128]{2,1,0:T(8,128)(2,1)S(1)}, bf16[9,128,128]{2,1,0:T(8,128)(2,1)}, u32[]{:S(2)}) copy-start(bf16[9,128,128]{2,1,0:T(8,128)(2,1)} %param.32) | copy-start | bytes 884740
  228.5 1.0 copy-start.1
  229.6 1.0 copy-start.2
  230.6 1.0 copy-start.3
  231.6 1.0 copy-start.4
  232.7 1.0 copy-start.5
  234.0 49.8 %copy-start.29 = (f32[128]{0:T(128)S(1)}, f32[128]{0:T(128)}, u32[]{:S(2)}) copy-start(f32[128]{0:T(128)} %param.34) | copy-start | bytes 1540
  234.0 49.7 %copy-start.30 = (f32[128]{0:T(128)S(1)}, f32[128]{0:T(128)}, u32[]{:S(2)}) copy-start(f32[128]{0:T(128)} %param.33) | copy-start | bytes 1540
  283.8 9.0 %copy-start.20 = (s32[16]{0:T(128)S(1)}, s32[16]{0:T(128)}, u32[]{:S(2)}) copy-start(s32[16]{0:T(128)} %get-tuple-element.30) | copy-start | bytes 196
  286.2 9.2 %copy-start.7 = (bf16[2048,128]{1,0:T(8,128)(2,1)}, bf16[2048,128]{1,0:T(8,128)(2,1)S(1)}, u32[]{:S(2)}) copy-start(bf16[2048,128]{1,0:T(8,128)(2,1)S(1)} %fusion.40) | copy-start | bytes 1572868
  287.6 5.8 %collective-permute-start.4 = (bf16[32,128]{1,0:T(8,128)(2,1)S(1)}, bf16[32,128]{1,0:T(8,128)(2,1)S(1)}, u32[]{:S(2)}, u32[]{:S(2)}) collective-permute-start(bf16[32,128]{1,0:T(8,128)(2,1)S(1)} %gather_fusion.22), channel_id=1, source_target_pairs={{0,1},{1,2},{2,3},{3,4},{4,5},{5,6},{6,7},{7,8},{8,9},{9,10},{10,1... | collective-permute-start | bytes 24584 | tf_op jit(solution)/shard_map/ppermute | solution.py:10
  288.2 5.8 %collective-permute-start.5 = (bf16[32,128]{1,0:T(8,128)(2,1)S(1)}, bf16[32,128]{1,0:T(8,128)(2,1)S(1)}, u32[]{:S(2)}, u32[]{:S(2)}) collective-permute-start(bf16[32,128]{1,0:T(8,128)(2,1)S(1)} %gather_fusion.23), channel_id=1, source_target_pairs={{0,15},{1,0},{2,1},{3,2},{4,3},{5,4},{6,5},{7,6},{8,7},{9,8},{10,9... | collective-permute-start | bytes 24584 | tf_op jit(solution)/shard_map/ppermute | solution.py:10
  317.1 50.6 %copy-start.21 = (f32[256]{0:T(256)S(1)}, f32[256]{0:T(256)}, u32[]{:S(2)}) copy-start(f32[256]{0:T(256)} %param.37) | copy-start | bytes 3076
  317.1 50.6 %copy-start.22 = (f32[256]{0:T(256)S(1)}, f32[256]{0:T(256)}, u32[]{:S(2)}) copy-start(f32[256]{0:T(256)} %param.36) | copy-start | bytes 3076
  318.8 55.8 %copy-start.19 = (s32[16]{0:T(128)S(1)}, s32[16]{0:T(128)}, u32[]{:S(2)}) copy-start(s32[16]{0:T(128)} %get-tuple-element.31) | copy-start | bytes 196
  370.1 5.9 %collective-permute-start.6 = (bf16[32,256]{1,0:T(8,128)(2,1)S(1)}, bf16[32,256]{1,0:T(8,128)(2,1)S(1)}, u32[]{:S(2)}, u32[]{:S(2)}) collective-permute-start(bf16[32,256]{1,0:T(8,128)(2,1)S(1)} %gather_fusion.33), channel_id=1, source_target_pairs={{0,1},{1,2},{2,3},{3,4},{4,5},{5,6},{6,7},{7,8},{8,9},{9,10},{10,1... | collective-permute-start | bytes 49160 | tf_op jit(solution)/shard_map/ppermute | solution.py:10
  370.2 5.9 %collective-permute-start.7 = (bf16[32,256]{1,0:T(8,128)(2,1)S(1)}, bf16[32,256]{1,0:T(8,128)(2,1)S(1)}, u32[]{:S(2)}, u32[]{:S(2)}) collective-permute-start(bf16[32,256]{1,0:T(8,128)(2,1)S(1)} %gather_fusion.34), channel_id=1, source_target_pairs={{0,15},{1,0},{2,1},{3,2},{4,3},{5,4},{6,5},{7,6},{8,7},{9,8},{10,9... | collective-permute-start | bytes 49160 | tf_op jit(solution)/shard_map/ppermute | solution.py:10
  393.0 2.0 copy-start.8
  395.6 1.0 copy-start.10
  395.9 1.0 copy-start.11
  397.1 49.2 %copy-start.23 = (f32[256]{0:T(256)S(1)}, f32[256]{0:T(256)}, u32[]{:S(2)}) copy-start(f32[256]{0:T(256)} %param.40) | copy-start | bytes 3076
  397.1 49.2 %copy-start.24 = (f32[256]{0:T(256)S(1)}, f32[256]{0:T(256)}, u32[]{:S(2)}) copy-start(f32[256]{0:T(256)} %param.39) | copy-start | bytes 3076
  446.3 8.1 %copy-start.18 = (s32[128]{0:T(128)S(1)}, s32[128]{0:T(128)}, u32[]{:S(2)}) copy-start(s32[128]{0:T(128)} %get-tuple-element.21) | copy-start | bytes 1540
  447.5 9.2 %copy-start.9 = (bf16[512,256]{1,0:T(8,128)(2,1)}, bf16[512,256]{1,0:T(8,128)(2,1)S(1)}, u32[]{:S(2)}) copy-start(bf16[512,256]{1,0:T(8,128)(2,1)S(1)} %fusion.60) | copy-start | bytes 786436
  447.5 10.2 %copy-start = (bf16[9,256,512]{2,1,0:T(8,128)(2,1)S(1)}, bf16[9,256,512]{2,1,0:T(8,128)(2,1)}, u32[]{:S(2)}) copy-start(bf16[9,256,512]{2,1,0:T(8,128)(2,1)} %param.41) | copy-start | bytes 7077892
  448.9 5.8 %collective-permute-start.8 = (bf16[16,256]{1,0:T(8,128)(2,1)S(1)}, bf16[16,256]{1,0:T(8,128)(2,1)S(1)}, u32[]{:S(2)}, u32[]{:S(2)}) collective-permute-start(bf16[16,256]{1,0:T(8,128)(2,1)S(1)} %gather_fusion.44), channel_id=1, source_target_pairs={{0,1},{1,2},{2,3},{3,4},{4,5},{5,6},{6,7},{7,8},{8,9},{9,10},{10,1... | collective-permute-start | bytes 24584 | tf_op jit(solution)/shard_map/ppermute | solution.py:10
  449.6 6.1 %collective-permute-start.9 = (bf16[16,256]{1,0:T(8,128)(2,1)S(1)}, bf16[16,256]{1,0:T(8,128)(2,1)S(1)}, u32[]{:S(2)}, u32[]{:S(2)}) collective-permute-start(bf16[16,256]{1,0:T(8,128)(2,1)S(1)} %gather_fusion.45), channel_id=1, source_target_pairs={{0,15},{1,0},{2,1},{3,2},{4,3},{5,4},{6,5},{7,6},{8,7},{9,8},{10,9... | collective-permute-start | bytes 24584 | tf_op jit(solution)/shard_map/ppermute | solution.py:10
  469.4 50.4 %copy-start.16 = (f32[512]{0:T(512)S(1)}, f32[512]{0:T(512)}, u32[]{:S(2)}) copy-start(f32[512]{0:T(512)} %param.43) | copy-start | bytes 6148
  469.4 50.4 %copy-start.17 = (f32[512]{0:T(512)S(1)}, f32[512]{0:T(512)}, u32[]{:S(2)}) copy-start(f32[512]{0:T(512)} %param.42) | copy-start | bytes 6148
